TPU v7x, 256 devices: a whole 4x4x8 slice. The times are simulated.
256 devices in a mesh: dp: 64 (over y, z, core), tensor: 4 (over x).
Axes of the slice: x: 4, y: 4, z: 8, core: 2. Of those that a mesh axis runs over, the one named last changes fastest.
Arguments:
- activations: bfloat16 [32768, 8192], P('dp', 'tensor'), may hold values from -2000 to 2000
- norm_gain: float32 [8192], replicated, may hold values from 0.5 to 12
- w_query: bfloat16 [8192, 4096], P('dp', 'tensor'), may hold values from -0.0625 to 0.0625
- w_key: bfloat16 [8192, 512], P('dp', 'tensor'), may hold values from -0.0625 to 0.0625
- w_value: bfloat16 [8192, 512], P('dp', 'tensor'), may hold values from -0.0625 to 0.0625
- lengths: int32 [128], replicated, may hold values from 128 to 256
- languages: int32 [128], replicated, may hold values from 0 to 29
- lang_caps: int32 [30], replicated, may hold values from 128 to 256
- dest_shard: int32 [128], replicated, may hold values from 0 to 63, as said below
Outputs:
- attended: bfloat16 [32768, 4096], P('dp', 'tensor')
Inputs may be any that keep to these rules, and one draw needn't show every extreme that they name: `dest_shard`: every data shard receives exactly 2 documents.
All inputs are finite; a program needn't handle non-finite values.
Results may differ from a plain program's by a relative error of at most 0.007.
The roundings to bfloat16 on the way count: a program that leaves them out, or rounds other values in their place, can miss the bound.
Values may be sent and summed in bfloat16 or wider, within the bound.
A program may use at most 128 MiB of HBM per device.

v0:
```python
import math
import jax
import jax.numpy as jnp
from jax import lax
from jax.sharding import PartitionSpec as P

HEAD_WIDTH = 128
rope_base = 500000.0
norm_eps = 1e-05


def rotary_embedding(vectors, token_positions):
    half_width = vectors.shape[-1] // 2
    steps_range = jnp.arange(half_width, dtype=jnp.float32)
    frequency = jnp.exp(steps_range * (-2.0 * math.log(rope_base) / vectors.shape[-1]))
    angles = token_positions[..., None, None] * frequency
    cosine = jnp.cos(angles)
    sine_table = jnp.sin(angles)
    first_half = vectors[..., :half_width]
    second_half = vectors[..., half_width:]
    return jnp.concatenate(
        [
            first_half * cosine - second_half * sine_table,
            second_half * cosine + first_half * sine_table,
        ],
        axis=-1,
    )


def project(source_rows, norm_gain, w_query, w_key, w_value):
    gathered = lax.all_gather(source_rows, "tensor", axis=1, tiled=True)
    widened = gathered.astype(jnp.float32)
    row_scale = lax.rsqrt(jnp.mean(widened * widened, axis=1, keepdims=True) + norm_eps)
    normed = (widened * row_scale * norm_gain).astype(jnp.bfloat16)
    pieces = (
        lax.all_gather(w_query, "dp", axis=0, tiled=True),
        lax.all_gather(w_key, "dp", axis=0, tiled=True),
        lax.all_gather(w_value, "dp", axis=0, tiled=True),
    )
    return tuple(
        (
            jnp.dot(normed, weight_piece, preferred_element_type=jnp.float32)
            for weight_piece in pieces
        )
    )


def rotate_round(query_part, key_portion, value_portion, token_positions, head_dim):
    total_rows = query_part.shape[0]
    rotated_query = rotary_embedding(
        query_part.reshape(total_rows, -1, head_dim), token_positions
    ).reshape(total_rows, -1)
    rotated_key = rotary_embedding(
        key_portion.reshape(total_rows, -1, head_dim), token_positions
    ).reshape(total_rows, -1)
    return jnp.concatenate([rotated_query, rotated_key, value_portion], axis=1).astype(jnp.bfloat16)


def attend(packed, doc_lengths, query_width, key_width, head_dim, doc_max):
    total_rows = packed.shape[0]
    doc_total = total_rows // doc_max
    value_head_rows = key_width // head_dim
    heads_per_group = query_width // key_width
    queries = packed[:, :query_width].reshape(
        doc_total, doc_max, value_head_rows, heads_per_group, head_dim
    )
    key_rows = packed[:, query_width : query_width + key_width].reshape(
        doc_total, doc_max, value_head_rows, head_dim
    )
    value_rows = packed[:, query_width + key_width :].reshape(
        doc_total, doc_max, value_head_rows, head_dim
    )
    scores = jnp.einsum(
        "jqhgd,jkhd->jhgqk", queries, key_rows, preferred_element_type=jnp.float32
    ) / math.sqrt(head_dim)
    order_range = jnp.arange(doc_max)
    causal = order_range[:, None] >= order_range[None, :]
    scores = jnp.where(causal, scores, -jnp.inf)
    row_peak = jnp.max(scores, axis=-1, keepdims=True)
    exponent = jnp.exp(scores - row_peak)
    probability = (exponent / jnp.sum(exponent, axis=-1, keepdims=True)).astype(jnp.bfloat16)
    blended = jnp.einsum(
        "jhgqk,jkhd->jqhgd", probability, value_rows, preferred_element_type=jnp.float32
    )
    blended = blended.reshape(doc_total, doc_max, query_width)
    row_valid = order_range[None, :] < doc_lengths[:, None]
    result = jnp.where(row_valid[..., None], blended, 0.0)
    return result.reshape(total_rows, query_width).astype(jnp.bfloat16)


def local(
    activations, norm_gain, w_query, w_key, w_value, lengths, languages, lang_caps, dest_shard
):
    shard_count = lax.axis_size("dp")
    my_shard = lax.axis_index("dp")
    doc_count = lengths.shape[0]
    token_rows = activations.shape[0]
    rows_peer = token_rows // doc_count
    doc_max = rows_peer * shard_count
    docs_here = doc_count // shard_count
    head_dim = HEAD_WIDTH
    query_width = w_query.shape[1]
    key_width = w_key.shape[1]
    language_table = jnp.arange(lang_caps.shape[0])
    cap_of_doc = jnp.sum(
        jnp.where(languages[:, None] == language_table[None, :], lang_caps[None, :], 0), axis=1
    )
    capped = jnp.minimum(lengths, cap_of_doc)
    doc_order = jnp.arange(doc_count)
    same_dest = dest_shard[:, None] == dest_shard[None, :]
    doc_rank = jnp.sum(
        (same_dest & (doc_order[None, :] < doc_order[:, None])).astype(jnp.int32), axis=1
    )
    target_slot = dest_shard * docs_here + doc_rank
    holder = jnp.sum(
        jnp.where(doc_order[:, None] == target_slot[None, :], doc_order[None, :], 0), axis=1
    )
    mine = lax.dynamic_slice_in_dim(holder, my_shard * docs_here, docs_here)
    doc_lengths = jnp.take(capped, mine)
    holder_grid = jnp.transpose(holder.reshape(shard_count, docs_here))
    send_index = (
        holder_grid[:, None, :] * rows_peer + jnp.arange(rows_peer)[None, :, None]
    ).reshape(-1)
    outgoing = jnp.take(activations, send_index, axis=0).reshape(
        docs_here, rows_peer, shard_count, -1
    )
    arrived = lax.all_to_all(outgoing, "dp", split_axis=2, concat_axis=2, tiled=True)
    moved_rows = arrived.reshape(docs_here * doc_max, -1)
    query_part, key_portion, value_portion = project(moved_rows, norm_gain, w_query, w_key, w_value)
    token_positions = jnp.tile(jnp.arange(doc_max), docs_here).astype(jnp.float32)
    packed = rotate_round(query_part, key_portion, value_portion, token_positions, head_dim)
    return attend(packed, doc_lengths, query_width, key_width, head_dim, doc_max)


def solution(mesh):
    return jax.shard_map(
        local,
        mesh=mesh,
        in_specs=(
            P("dp", "tensor"),
            P(),
            P("dp", "tensor"),
            P("dp", "tensor"),
            P("dp", "tensor"),
            P(),
            P(),
            P(),
            P(),
        ),
        out_specs=P("dp", "tensor"),
        check_vma=False,
    )
```

profile of v0, /device:TPU:1, one launch (start us, length us, event | category | flops | bytes accessed | tf_op | source)
XLA Modules:
  0.0 453.7 jit_solution(18384676850716704676)
XLA Ops:
  6.5 0.0 copy-start
  6.5 0.0 all-gather.5.cloned.1.call-start
  6.5 1.0 convert_reduce_fusion
  7.5 0.7 multiply_add_fusion
  8.2 0.1 select_reduce_fusion
  8.3 0.1 mul.188
  8.5 0.1 copy.35
  8.6 0.1 add.84
  8.7 0.1 copy.36
  8.8 0.0 copy-done
  8.8 3.3 gather_fusion.1
  12.2 3.8 copy_select_fusion
  16.0 64.1 %all_to_all.5 = bf16[2,4,64,2048]{3,1,0,2:T(4,128)(2,1)S(1)} all-to-all(bf16[2,4,64,2048]{3,1,0,2:T(4,128)(2,1)S(1)} %copy_select_fusion), channel_id=1, replica_groups=mesh['dp'=64,'tensor'=4] {'dp'}, dimensions={2} | all-to-all | bytes 4194304 | tf_op jit(solution)/shard_map/all_to_all | solution.py:127
  80.1 0.0 copy-start.2
  80.1 0.0 copy-start.3
  80.1 0.0 copy-start.4
  80.1 2.5 copy.38
  82.7 0.0 all-gather.5.cloned.1.call-update
  82.7 0.0 all-gather.9.cloned.1.call-start
  82.7 0.7 all-gather.9.cloned.1.call-update
  83.4 0.0 all-gather.7.cloned.1.call-start
  83.5 0.7 all-gather.7.cloned.1.call-update
  84.2 0.0 all-gather.11.cloned.1.call-start
  84.2 0.5 all-gather.11.cloned.1.call-update
  84.8 0.0 copy-done.2
  84.8 0.0 copy-done.3
  84.8 0.1 select_reduce_fusion.1
  84.9 0.0 copy-done.4
  84.9 0.1 compare_select_fusion.2
  85.0 0.6 gather_fusion
  85.6 0.1 and_select_fusion
  85.7 0.1 iota_compare_fusion.4
  85.8 1.0 multiply_cosine_fusion
  86.8 0.0 copy-start.1
  86.8 77.9 %all-gather.5.cloned.1.call-done = bf16[512,8192]{1,0:T(8,128)(2,1)} async-done(((bf16[512,2048]{1,0:T(8,128)(2,1)}), bf16[512,8192]{1,0:T(8,128)(2,1)}) %all-gather.5.cloned.1.call-update) | async-done | bytes 8388624 | tf_op jit(solution)/shard_map/all_gather | solution.py:31
  164.7 5.1 %fusion = f32[512]{0:T(512)S(1)} fusion(bf16[512,8192]{1,0:T(8,128)(2,1)} %all-gather.5.cloned.1.call-done), kind=kLoop, calls=%fused_computation.4 | loop fusion | flops 12582400 | bytes 8390656 | tf_op jit(solution)/shard_map/reduce_sum | solution.py:33
  169.8 76.8 %all-gather.9.cloned.1.call-done = bf16[8192,128]{1,0:T(8,128)(2,1)} async-done(((bf16[128,128]{1,0:T(8,128)(2,1)}), bf16[8192,128]{1,0:T(8,128)(2,1)}) %all-gather.9.cloned.1.call-update) | async-done | bytes 2097168 | tf_op jit(solution)/shard_map/all_gather | solution.py:37
  246.6 0.0 copy-done.1
  246.6 6.5 %convolution_bitcast_fusion.1 = f32[512,1,128]{0,2,1:T(8,128)S(1)} fusion(bf16[8192,128]{1,0:T(8,128)(2,1)} %all-gather.9.cloned.1.call-done, bf16[512,8192]{1,0:T(8,128)(2,1)} %all-gather.5.cloned.1.call-done, f32[8192]{0:T(1024)S(1)} %copy-done.1, f32[512]{0:T(512)S(1)} %add_rsqrt_fusion), kind=kOutput, calls=%fused_computation.22 | convolution fusion | flops 1090519040 | bytes 10782720 | tf_op jit(solution)/shard_map/dot_general | solution.py:42
  253.1 0.6 fusion.19
  253.7 0.1 copy.49
  253.8 70.6 %all-gather.7.cloned.1.call-done = bf16[8192,128]{1,0:T(8,128)(2,1)} async-done(((bf16[128,128]{1,0:T(8,128)(2,1)}), bf16[8192,128]{1,0:T(8,128)(2,1)}) %all-gather.7.cloned.1.call-update) | async-done | bytes 2097168 | tf_op jit(solution)/shard_map/all_gather | solution.py:38
  324.4 6.4 %convolution_convert_fusion = bf16[512,128]{1,0:T(8,128)(2,1)S(1)} fusion(bf16[8192,128]{1,0:T(8,128)(2,1)} %all-gather.7.cloned.1.call-done, bf16[512,8192]{1,0:T(8,128)(2,1)} %all-gather.5.cloned.1.call-done, f32[8192]{0:T(1024)S(1)} %copy-done.1, f32[512]{0:T(512)S(1)} %add_rsqrt_fusion), kind=kOutput, calls=%fused_computation.23 | convolution fusion | flops 1090584576 | bytes 10651648 | tf_op jit(solution)/shard_map/dot_general | solution.py:42
  330.8 93.0 %all-gather.11.cloned.1.call-done = bf16[8192,1024]{1,0:T(8,128)(2,1)} async-done(((bf16[128,1024]{1,0:T(8,128)(2,1)}), bf16[8192,1024]{1,0:T(8,128)(2,1)}) %all-gather.11.cloned.1.call-update) | async-done | bytes 16777232 | tf_op jit(solution)/shard_map/all_gather | solution.py:36
  423.8 14.5 %convolution_bitcast_fusion = f32[64,8,8,128]{3,1,2,0:T(8,128)S(1)} fusion(bf16[8192,1024]{1,0:T(8,128)(2,1)} %all-gather.11.cloned.1.call-done, bf16[512,8192]{1,0:T(8,128)(2,1)} %all-gather.5.cloned.1.call-done, f32[8192]{0:T(1024)S(1)} %copy-done.1, f32[512]{0:T(512)S(1)} %add_rsqrt_fusion), kind=kOutput, calls=%fused_computation.21 | convolution fusion | flops 8606711808 | bytes 27297792 | tf_op jit(solution)/shard_map/dot_general | solution.py:42
  438.3 0.5 copy.51
  438.8 0.9 subtract_convert_fusion
  439.7 0.6 pad_maximum_fusion
  440.3 0.8 fusion.4
  441.0 0.9 fusion.3
  441.9 2.3 fusion.9
  444.2 1.7 copy.43
  445.9 1.2 fusion.5
  (14 shorter events, 0.1 us)
Async XLA Ops:
  6.5 2.3 copy-start
  6.5 158.2 %all-gather.5.cloned.1.call-start = ((), (), s32[]{:S(2)}) async-start(), calls=%async_computation.1 | async-start | bytes 10485760 | tf_op jit(solution)/shard_map/all_gather | solution.py:31
  80.1 4.6 %copy-start.2 = (s32[30]{0:T(128)S(1)}, s32[30]{0:T(128)}, u32[]{:S(2)}) copy-start(s32[30]{0:T(128)} %param.16) | copy-start | bytes 364
  80.1 4.6 %copy-start.3 = (s32[128]{0:T(128)S(1)}, s32[128]{0:T(128)}, u32[]{:S(2)}) copy-start(s32[128]{0:T(128)} %param.15) | copy-start | bytes 1540
  80.1 4.7 %copy-start.4 = (s32[128]{0:T(128)S(1)}, s32[128]{0:T(128)}, u32[]{:S(2)}) copy-start(s32[128]{0:T(128)} %param.14) | copy-start | bytes 1540
  82.7 164.0 %all-gather.9.cloned.1.call-start = ((), (), s32[]{:S(2)}) async-start(), calls=%async_computation.3 | async-start | bytes 2129920 | tf_op jit(solution)/shard_map/all_gather | solution.py:37
  83.4 241.0 %all-gather.7.cloned.1.call-start = ((), (), s32[]{:S(2)}) async-start(), calls=%async_computation.2 | async-start | bytes 2129920 | tf_op jit(solution)/shard_map/all_gather | solution.py:38
  84.2 339.6 %all-gather.11.cloned.1.call-start = ((), (), s32[]{:S(2)}) async-start(), calls=%async_computation.4 | async-start | bytes 17039360 | tf_op jit(solution)/shard_map/all_gather | solution.py:36
  86.8 159.8 %copy-start.1 = (f32[8192]{0:T(1024)S(1)}, f32[8192]{0:T(1024)}, u32[]{:S(2)}) copy-start(f32[8192]{0:T(1024)} %param.10) | copy-start | bytes 98308
Sparse Core Ops, SparseCore 0:
  82.8 81.8 all-gather.4
  167.5 79.0 all-gather.8
  249.4 74.9 all-gather.6
  327.1 96.6 all-gather.10
where the time goes:
time: 454 us
  waiting for transfers between devices  320 us (70%)
  blocking collectives  64.1 us (14%)
  matrix products  30.4 us (7%)
  other arithmetic  16.2 us (4%)
  between operations  13.3 us (3%)
  local copies, waits for them, and re-layouts  9.25 us (2%)
    all_gather x1, waiting for transfers between devices, project(): lax.all_gather(w_query, 'dp', axis=0, tiled=True)  93 us
    all_gather x1, waiting for transfers between devices, project(): gathered = lax.all_gather(source_rows, 'tensor', axis=1, tiled=True)  77.9 us
    all_gather x1, waiting for transfers between devices, project(): lax.all_gather(w_key, 'dp', axis=0, tiled=True)  76.8 us
    all_gather x1, waiting for transfers between devices, project(): lax.all_gather(w_value, 'dp', axis=0, tiled=True)  70.6 us
    all_to_all x1, blocking collectives, local(): lax.all_to_all(outgoing, 'dp', split_axis=2, concat_axis=2, tiled=True)  64.1 us
    dot_general x3, matrix products, project(): jnp.dot(normed, weight_piece, preferred_element_type=jnp.float32)  27.4 us
  transfers between devices with their start and end apart: 4, of which 4 were waited for; matrix products, arithmetic and copies ran while one was open for 5% of the time, Pallas kernels for 0%

commit v1 on v0

--- a/solution.py
+++ b/solution.py
@@ -7,6 +7,15 @@
 HEAD_WIDTH = 128
 rope_base = 500000.0
 norm_eps = 1e-05
+
+
+def prepare_roads_on_mesh(shard_in):
+    num = lax.axis_size("dp")
+    runs = list(map(lambda h: num if h == 0 else 1, range(shard_in.ndim)))
+    state_now = lax.all_to_all(
+        jnp.tile(shard_in, runs), axis_name="dp", split_axis=0, concat_axis=0, tiled=True
+    )
+    return state_now
 
 
 def rotary_embedding(vectors, token_positions):
@@ -34,7 +43,7 @@
     normed = (widened * row_scale * norm_gain).astype(jnp.bfloat16)
     pieces = (
         lax.all_gather(w_query, "dp", axis=0, tiled=True),
-        lax.all_gather(w_key, "dp", axis=0, tiled=True),
+        prepare_roads_on_mesh(w_key),
         lax.all_gather(w_value, "dp", axis=0, tiled=True),
     )
     return tuple(

time: 454 us -> 376 us (0.83)
  waiting for transfers between devices: 320 us -> 235 us
  starting transfers between devices: 0.12 us -> 6.11 us
    all_gather x1 -> x0, waiting for transfers between devices: 76.8 us -> none  [project(): lax.all_gather(w_key, 'dp', axis=0, tiled=True)]
    all_gather x1, waiting for transfers between devices: 77.9 us -> 70.6 us  [project(): gathered = lax.all_gather(source_rows, 'tensor', axis=1, tiled=True)]
    all_to_all x0 -> x1, starting transfers between devices: none -> 6.03 us  [prepare_roads_on_mesh(): lax.all_to_all(jnp.tile(shard_in, runs), axis_name='dp', split_axis=0, co...]
  transfers between devices with their start and end apart: 4 -> 4, of which waited for: 4 -> 3; matrix products, arithmetic and copies ran while one was open for 5% -> 6% of each run, Pallas kernels for 0% -> 0%
where the time goes in v1:
time: 376 us
  waiting for transfers between devices  235 us (62%)
  blocking collectives  64.1 us (17%)
  matrix products  30.6 us (8%)
  other arithmetic  16.2 us (4%)
  between operations  13.3 us (4%)
  local copies, waits for them, and re-layouts  11 us (3%)
  starting transfers between devices  6.11 us (2%)
    all_gather x1, waiting for transfers between devices, project(): lax.all_gather(w_query, 'dp', axis=0, tiled=True)  93.1 us
    all_gather x1, waiting for transfers between devices, project(): gathered = lax.all_gather(source_rows, 'tensor', axis=1, tiled=True)  70.6 us
    all_gather x1, waiting for transfers between devices, project(): lax.all_gather(w_value, 'dp', axis=0, tiled=True)  69.6 us
    all_to_all x1, blocking collectives, local(): lax.all_to_all(outgoing, 'dp', split_axis=2, concat_axis=2, tiled=True)  64.1 us
    dot_general x3, matrix products, project(): jnp.dot(normed, weight_piece, preferred_element_type=jnp.float32)  27.6 us
  transfers between devices with their start and end apart: 4, of which 3 were waited for; matrix products, arithmetic and copies ran while one was open for 6% of the time, Pallas kernels for 0%

profile of v1, /device:TPU:1, one launch (start us, length us, event | category | flops | bytes accessed | tf_op | source)
XLA Modules:
  0.0 376.2 jit_solution(10887657832484510054)
XLA Ops:
  6.5 0.0 copy-start
  6.5 0.0 all-gather.4.cloned.1.call-start
  6.5 1.0 convert_reduce_fusion
  7.5 0.7 multiply_add_fusion
  8.2 0.1 select_reduce_fusion
  8.3 0.1 mul.188
  8.5 0.1 copy.35
  8.6 0.1 add.84
  8.7 0.1 copy.36
  8.8 0.0 copy-done
  8.8 3.3 gather_fusion.1
  12.2 3.8 %copy_select_fusion = bf16[2,4,64,2048]{3,1,0,2:T(4,128)(2,1)S(1)} fusion(bf16[2,4,64,2048]{3,2,1,0:T(8,128)(2,1)} %bitcast.61, pred[2,4,64]{1,0,2:T(4,128)(4,1)S(1)} %copy.36), kind=kLoop, calls=%fused_computation.16 | loop fusion | flops 1048576 | bytes 4194816 | tf_op jit(solution)/shard_map/jit(_take)/select_n | solution.py:133
  16.0 64.1 %all_to_all.14 = bf16[2,4,64,2048]{3,1,0,2:T(4,128)(2,1)S(1)} all-to-all(bf16[2,4,64,2048]{3,1,0,2:T(4,128)(2,1)S(1)} %copy_select_fusion), channel_id=1, replica_groups=mesh['dp'=64,'tensor'=4] {'dp'}, dimensions={2} | all-to-all | bytes 4194304 | tf_op jit(solution)/shard_map/all_to_all | solution.py:136
  80.1 0.0 copy-start.1
  80.1 2.5 copy.38
  82.6 0.0 copy-start.3
  82.6 0.0 copy-start.4
  82.6 0.0 copy-start.5
  82.6 0.0 all-gather.4.cloned.1.call-update
  82.6 0.0 all-gather.6.cloned.1.call-start
  82.7 0.7 all-gather.6.cloned.1.call-update
  83.4 0.0 all-gather.8.cloned.1.call-start
  83.4 0.7 all-gather.8.cloned.1.call-update
  84.1 0.0 copy-done.1
  84.1 1.8 tile.2
  86.0 6.0 %all-to-all-start.1 = ((bf16[64,128,128]{2,1,0:T(8,128)(2,1)}), bf16[64,128,128]{2,1,0:T(8,128)(2,1)}, u32[]{:S(2)}, u32[]{:S(2)}) async-start(bf16[64,128,128]{2,1,0:T(8,128)(2,1)} %tile.2), calls=%async_computation.1 | async-start | bytes 4194304 | tf_op jit(solution)/shard_map/all_to_all | solution.py:15
  92.0 0.0 copy-done.3
  92.0 0.0 copy-done.4
  92.0 0.1 select_reduce_fusion.1
  92.1 0.0 copy-done.5
  92.1 0.1 compare_select_fusion.2
  92.2 0.6 gather_fusion
  92.9 0.1 and_select_fusion
  93.0 0.1 iota_compare_fusion.4
  93.1 1.0 multiply_cosine_fusion
  94.1 0.0 copy-start.2
  94.1 70.6 %all-gather.4.cloned.1.call-done = bf16[512,8192]{1,0:T(8,128)(2,1)} async-done(((bf16[512,2048]{1,0:T(8,128)(2,1)}), bf16[512,8192]{1,0:T(8,128)(2,1)}) %all-gather.4.cloned.1.call-update) | async-done | bytes 8388624 | tf_op jit(solution)/shard_map/all_gather | solution.py:40
  164.7 5.1 %fusion = f32[512]{0:T(512)S(1)} fusion(bf16[512,8192]{1,0:T(8,128)(2,1)} %all-gather.4.cloned.1.call-done), kind=kLoop, calls=%fused_computation.4 | loop fusion | flops 12582400 | bytes 8390656 | tf_op jit(solution)/shard_map/reduce_sum | solution.py:42
  169.8 0.0 all-to-all-done.1
  169.8 0.0 copy-done.2
  169.8 6.5 %convolution_bitcast_fusion.1 = f32[512,1,128]{0,2,1:T(8,128)S(1)} fusion(bf16[8192,128]{1,0:T(8,128)(2,1)} %bitcast.6, bf16[512,8192]{1,0:T(8,128)(2,1)} %all-gather.4.cloned.1.call-done, f32[8192]{0:T(1024)S(1)} %copy-done.2, f32[512]{0:T(512)S(1)} %add_rsqrt_fusion), kind=kOutput, calls=%fused_computation.22 | convolution fusion | flops 1090519040 | bytes 10782720 | tf_op jit(solution)/shard_map/dot_general | solution.py:51
  176.3 0.6 fusion.19
  176.9 0.1 copy.49
  177.0 69.6 %all-gather.6.cloned.1.call-done = bf16[8192,128]{1,0:T(8,128)(2,1)} async-done(((bf16[128,128]{1,0:T(8,128)(2,1)}), bf16[8192,128]{1,0:T(8,128)(2,1)}) %all-gather.6.cloned.1.call-update) | async-done | bytes 2097168 | tf_op jit(solution)/shard_map/all_gather | solution.py:47
  246.6 6.4 %convolution_convert_fusion = bf16[512,128]{1,0:T(8,128)(2,1)S(1)} fusion(bf16[8192,128]{1,0:T(8,128)(2,1)} %all-gather.6.cloned.1.call-done, bf16[512,8192]{1,0:T(8,128)(2,1)} %all-gather.4.cloned.1.call-done, f32[8192]{0:T(1024)S(1)} %copy-done.2, f32[512]{0:T(512)S(1)} %add_rsqrt_fusion), kind=kOutput, calls=%fused_computation.23 | convolution fusion | flops 1090584576 | bytes 10651648 | tf_op jit(solution)/shard_map/dot_general | solution.py:51
  253.0 93.1 %all-gather.8.cloned.1.call-done = bf16[8192,1024]{1,0:T(8,128)(2,1)} async-done(((bf16[128,1024]{1,0:T(8,128)(2,1)}), bf16[8192,1024]{1,0:T(8,128)(2,1)}) %all-gather.8.cloned.1.call-update) | async-done | bytes 16777232 | tf_op jit(solution)/shard_map/all_gather | solution.py:45
  346.1 14.7 %convolution_bitcast_fusion = f32[64,8,8,128]{3,1,2,0:T(8,128)S(1)} fusion(bf16[8192,1024]{1,0:T(8,128)(2,1)} %all-gather.8.cloned.1.call-done, bf16[512,8192]{1,0:T(8,128)(2,1)} %all-gather.4.cloned.1.call-done, f32[8192]{0:T(1024)S(1)} %copy-done.2, f32[512]{0:T(512)S(1)} %add_rsqrt_fusion), kind=kOutput, calls=%fused_computation.21 | convolution fusion | flops 8606711808 | bytes 27297792 | tf_op jit(solution)/shard_map/dot_general | solution.py:51
  360.9 0.5 copy.51
  361.3 0.9 subtract_convert_fusion
  362.2 0.6 pad_maximum_fusion
  362.8 0.8 fusion.4
  363.6 0.9 fusion.3
  364.4 2.3 fusion.9
  366.7 1.7 copy.43
  368.4 1.2 fusion.5
  (14 shorter events, 0.1 us)
Async XLA Ops:
  6.5 2.3 copy-start
  6.5 158.2 %all-gather.4.cloned.1.call-start = ((), (), s32[]{:S(2)}) async-start(), calls=%async_computation.2 | async-start | bytes 10485760 | tf_op jit(solution)/shard_map/all_gather | solution.py:40
  80.1 4.0 %copy-start.1 = (bf16[128,128]{1,0:T(8,128)(2,1)S(1)}, bf16[128,128]{1,0:T(8,128)(2,1)}, u32[]{:S(2)}) copy-start(bf16[128,128]{1,0:T(8,128)(2,1)} %param.12) | copy-start | bytes 98308
  82.6 9.4 %copy-start.3 = (s32[30]{0:T(128)S(1)}, s32[30]{0:T(128)}, u32[]{:S(2)}) copy-start(s32[30]{0:T(128)} %param.16) | copy-start | bytes 364
  82.6 9.4 %copy-start.4 = (s32[128]{0:T(128)S(1)}, s32[128]{0:T(128)}, u32[]{:S(2)}) copy-start(s32[128]{0:T(128)} %param.15) | copy-start | bytes 1540
  82.6 9.5 %copy-start.5 = (s32[128]{0:T(128)S(1)}, s32[128]{0:T(128)}, u32[]{:S(2)}) copy-start(s32[128]{0:T(128)} %param.14) | copy-start | bytes 1540
  82.6 164.0 %all-gather.6.cloned.1.call-start = ((), (), s32[]{:S(2)}) async-start(), calls=%async_computation.3 | async-start | bytes 2129920 | tf_op jit(solution)/shard_map/all_gather | solution.py:47
  83.4 262.7 %all-gather.8.cloned.1.call-start = ((), (), s32[]{:S(2)}) async-start(), calls=%async_computation.4 | async-start | bytes 17039360 | tf_op jit(solution)/shard_map/all_gather | solution.py:45
  86.0 83.9 %all-to-all-start.1 = ((bf16[64,128,128]{2,1,0:T(8,128)(2,1)}), bf16[64,128,128]{2,1,0:T(8,128)(2,1)}, u32[]{:S(2)}, u32[]{:S(2)}) async-start(bf16[64,128,128]{2,1,0:T(8,128)(2,1)} %tile.2), calls=%async_computation.1 | async-start | bytes 4194304 | tf_op jit(solution)/shard_map/all_to_all | solution.py:15
  94.1 75.7 %copy-start.2 = (f32[8192]{0:T(1024)S(1)}, f32[8192]{0:T(1024)}, u32[]{:S(2)}) copy-start(f32[8192]{0:T(1024)} %param.10) | copy-start | bytes 98308
Sparse Core Ops, SparseCore 0:
  82.8 81.8 all-gather.3
  167.5 79.0 all-gather.5
  249.4 96.6 all-gather.7
